TPU v7x, 32 devices: a whole 2x2x4 slice. The times are simulated.
32 devices in a mesh: ctx: 8 (over z, y), head: 4 (over x, core).
Axes of the slice: x: 2, y: 2, z: 4, core: 2. Of those that a mesh axis runs over, the one named last changes fastest.
Arguments:
- tokens: bfloat16 [2048, 6144], P('ctx'), may hold values from -6 to 6
- query_heads: bfloat16 [2048, 4096], P('ctx', 'head'), may hold values from -6 to 6
- key_heads: bfloat16 [2048, 4096], P('ctx', 'head'), may hold values from -6 to 6
- w_value: bfloat16 [6144, 4096], P('ctx', 'head'), may hold values from -0.078125 to 0.078125
- norm_gain: float32 [4096], P('head'), may hold values from 0.5 to 1.5
Outputs:
- attn_out: bfloat16 [2048, 4096], P('ctx', 'head')
All inputs are finite; a program needn't handle non-finite values.
Results may differ from a plain program's by a relative error of at most 0.0054.
Values may be sent and summed in bfloat16 or wider, within the bound.
A program may use at most 128 MiB of HBM per device.

v0:
```python
import jax
import jax.numpy as jnp
from jax import lax
from jax.sharding import PartitionSpec as P

HD = 128
BLOCK = 256


def prefix(part, axis, combine, identity):
    place = lax.axis_index(axis)
    gathered = lax.all_gather(part, axis)
    state = jnp.zeros_like(part) + jnp.asarray(identity, part.dtype)

    def one(lap, state):
        return combine(state, lax.dynamic_index_in_dim(gathered, lap, 0, False))

    return lax.fori_loop(0, place, one, state)


def add_states(earlier, later):
    return earlier + later


def on_device(tokens, query_heads, key_heads, w_value, norm_gain):
    token_count = tokens.shape[0]
    width = w_value.shape[1]
    heads_here = width // HD
    full_weight = lax.all_gather(w_value, "ctx", axis=0, tiled=True)
    pre_value = jnp.dot(tokens, full_weight, preferred_element_type=jnp.float32)
    value_heads = jax.nn.silu(pre_value).astype(jnp.bfloat16)
    block_count = token_count // BLOCK
    block_shape = (block_count, BLOCK, heads_here, HD)
    shaped_q = query_heads.reshape(block_shape)
    shaped_k = key_heads.reshape(block_shape)
    shaped_v = value_heads.reshape(block_shape)
    local_states = jnp.einsum(
        "bshd,bshe->bhde", shaped_k, shaped_v, preferred_element_type=jnp.float32
    )
    device_state = jnp.sum(local_states, axis=0)
    running_sum = jnp.cumsum(local_states, axis=0)
    before_block = jnp.concatenate([jnp.zeros_like(local_states), running_sum[:-1]], axis=0)
    earlier = prefix(device_state, "ctx", add_states, jnp.zeros_like(device_state))
    prefix_state = earlier[None] + before_block
    inter = jnp.einsum(
        "bshd,bhde->bshe",
        shaped_q.astype(jnp.float32),
        prefix_state,
        precision=lax.Precision.HIGHEST,
    )
    scores = jnp.einsum("bshd,bthd->bhst", shaped_q, shaped_k, preferred_element_type=jnp.float32)
    causal = jnp.tril(jnp.ones((BLOCK, BLOCK), jnp.bool_))
    scores = jnp.where(causal[None, None], scores, jnp.float32(0.0)).astype(jnp.bfloat16)
    intra = jnp.einsum("bhst,bthd->bshd", scores, shaped_v, preferred_element_type=jnp.float32)
    attended = (inter + intra).reshape(token_count, heads_here, HD)
    mean_square = jnp.mean(attended * attended, axis=2, keepdims=True)
    normed = attended * lax.rsqrt(mean_square + 1e-05) * norm_gain.reshape(1, heads_here, HD)
    return normed.reshape(token_count, width).astype(jnp.bfloat16)


def solution(mesh):
    return jax.shard_map(
        on_device,
        mesh=mesh,
        in_specs=(P("ctx", None), P("ctx", "head"), P("ctx", "head"), P("ctx", "head"), P("head")),
        out_specs=P("ctx", "head"),
        check_vma=False,
    )
```

profile of v0, /device:TPU:31, one launch (start us, length us, event | category | flops | bytes accessed | tf_op | source)
XLA Modules:
  0.0 305.0 jit_solution(7786030738092201563)
XLA Ops:
  6.5 0.0 copy-start
  6.5 0.0 all-gather.4.cloned.1.call-start
  6.5 0.7 all-gather.4.cloned.1.call-update
  7.3 0.0 all-gather.6.cloned.1.call-start
  7.3 2.2 copy.24
  9.6 174.7 %all-gather.4.cloned.1.call-done = bf16[6144,1024]{1,0:T(8,128)(2,1)} async-done(((bf16[768,1024]{1,0:T(8,128)(2,1)}), bf16[6144,1024]{1,0:T(8,128)(2,1)}) %all-gather.4.cloned.1.call-update) | async-done | bytes 12582928 | tf_op jit(solution)/shard_map/all_gather | solution.py:29
  184.3 0.0 copy-done
  184.3 8.9 %multiply_convert_fusion = bf16[256,1024]{1,0:T(8,128)(2,1)} fusion(bf16[256,6144]{1,0:T(8,128)(2,1)S(1)} %copy-done, bf16[6144,1024]{1,0:T(8,128)(2,1)} %all-gather.4.cloned.1.call-done), kind=kOutput, calls=%fused_computation.11 | convolution fusion | flops 3222536192 | bytes 16252928 | tf_op jit(solution)/shard_map/dot_general | solution.py:30
  193.2 2.0 copy.23
  195.2 2.3 convolution_bitcast_fusion
  197.5 2.0 copy.15
  199.5 0.0 all-gather.6.cloned.1.call-update
  199.6 71.8 %all-gather.6.cloned.1.call-done = f32[64,128,128]{2,1,0:T(8,128)} async-done(((f32[8,128,128]{2,1,0:T(8,128)}), f32[64,128,128]{2,1,0:T(8,128)}) %all-gather.6.cloned.1.call-update) | async-done | bytes 4194320 | tf_op jit(solution)/shard_map/all_gather | solution.py:12
  271.4 0.8 broadcast_in_dim.21
  272.3 14.3 %while.10 = (s32[]{:T(128)}, f32[8,128,128]{2,1,0:T(8,128)}, s32[]{:T(128)}, f32[8,8,128,128]{3,2,1,0:T(8,128)}, s32[]{:T(128)}, /*index=5*/s32[]{:T(128)}, s32[]{:T(128)}) while((s32[]{:T(128)}, f32[8,128,128]{2,1,0:T(8,128)}, s32[]{:T(128)}, f32[8,8,128,128]{3,2,1,0:T(8,128)}, s32[]{:T(128)}, /*index=5*/s32[]{:T(128)}, s32[]{:T(128)}) %tuple.27), condition=%wide.region_1.2_spmd, body=%wide.region_0.1_spmd.sunk | while | flops 131077 | bytes 1572979 | solution.py:18
  272.3 2.0 bitcast_add_fusion.2
  274.3 2.0 bitcast_add_fusion.2
  276.3 2.0 bitcast_add_fusion.2
  278.4 2.0 bitcast_add_fusion.2
  280.4 2.0 bitcast_add_fusion.2
  282.5 2.0 bitcast_add_fusion.2
  284.5 2.0 bitcast_add_fusion.2
  286.6 2.9 fusion.9
  289.4 0.0 copy-start.1
  289.4 3.5 %fusion.4 = (f32[256,8]{0,1:T(8,128)S(1)}, f32[8,128,256]{2,1,0:T(8,128)}) fusion(f32[8,128,256]{2,1,0:T(8,128)} %fusion.9, bf16[256,8,128]{0,2,1:T(8,128)(2,1)} %bitcast.51, bf16[256,8,128]{0,2,1:T(8,128)(2,1)} %bitcast.49, pred[256,256]{1,0:T(8,128)(4,1)S(1)} %iota_compare_fusion, bf16[256,1024]{1,0:T(8,128)(2,1)} %param.8), kind=kOutput, calls=%fused_computation.9 | convolution fusion | flops 270268416 | bytes 3743744 | tf_op jit(solution)/shard_map/bhst,bthd->bshd/dot_general | solution.py:54
  292.9 0.1 copy.19
  293.0 2.5 copy.20
  295.6 0.3 mul.30
  295.9 0.0 copy-done.1
  295.9 2.3 fusion.3
  (2 shorter events, 0.0 us)
Async XLA Ops:
  6.5 177.8 %copy-start = (bf16[256,6144]{1,0:T(8,128)(2,1)S(1)}, bf16[256,6144]{1,0:T(8,128)(2,1)}, u32[]{:S(2)}) copy-start(bf16[256,6144]{1,0:T(8,128)(2,1)} %param.7) | copy-start | bytes 9437188
  6.5 177.8 %all-gather.4.cloned.1.call-start = ((), (), s32[]{:S(2)}) async-start(), calls=%async_computation | async-start | bytes 14155776 | tf_op jit(solution)/shard_map/all_gather | solution.py:29
  7.3 264.2 %all-gather.6.cloned.1.call-start = ((), (), s32[]{:S(2)}) async-start(), calls=%async_computation.1 | async-start | bytes 4718592 | tf_op jit(solution)/shard_map/all_gather | solution.py:12
  289.4 6.5 %copy-start.1 = (f32[1024]{0:T(1024)S(1)}, f32[1024]{0:T(1024)}, u32[]{:S(2)}) copy-start(f32[1024]{0:T(1024)} %param.11) | copy-start | bytes 12292
Sparse Core Ops, SparseCore 0:
  9.5 174.6 all-gather.3
  199.7 71.6 all-gather.5
where the time goes:
time: 306 us; the launch traced here: 305 us
  waiting for transfers between devices  247 us (81%)
  matrix products  17.5 us (6%)
  other arithmetic  16.7 us (5%)
  between operations  13.4 us (4%)
  local copies, waits for them, and re-layouts  10.2 us (3%)
    all_gather x1, waiting for transfers between devices, on_device(): full_weight = lax.all_gather(w_value, 'ctx', axis=0, tiled=True)  175 us
    all_gather x1, waiting for transfers between devices, prefix(): gathered = lax.all_gather(part, axis)  71.8 us
    add x7, other arithmetic, add_states(): return earlier + later  14.3 us
    dot_general x1, matrix products, on_device(): pre_value = jnp.dot(tokens, full_weight, preferred_element_type=jnp.float32)  8.86 us
  transfers between devices with their start and end apart: 2, of which 2 were waited for; matrix products, arithmetic and copies ran while one was open for 1% of the time, Pallas kernels for 0%

commit v1 on v0

--- a/solution.py
+++ b/solution.py
@@ -1,7 +1,16 @@
+import functools
+
 import jax
 import jax.numpy as jnp
 from jax import lax
+from jax.experimental import pallas as pl
+from jax.experimental.pallas import tpu as pltpu
 from jax.sharding import PartitionSpec as P
+
+MESH = pl.DeviceIdType.MESH
+F32 = jnp.float32
+BF16 = jnp.bfloat16
+CW = 256
 
 HD = 128
 BLOCK = 256
@@ -22,7 +31,7 @@
     return earlier + later
 
 
-def on_device(tokens, query_heads, key_heads, w_value, norm_gain):
+def plain(tokens, query_heads, key_heads, w_value, norm_gain):
     token_count = tokens.shape[0]
     width = w_value.shape[1]
     heads_here = width // HD
@@ -58,9 +67,260 @@
     return normed.reshape(token_count, width).astype(jnp.bfloat16)
 
 
+def fused_kernel(
+    nz, chunks, tokens, query, key, weight, gain, out,
+    tok, wbuf, p_send, p_recv, acc, scores, value, att, state, state_in, t_send, t_recv, pre_send, pre,
+    local_sem, w_ss, w_rs, tok_ss, tok_rs, x_ss, x_rs, core_ss, core_rs, p_ss, p_rs,
+    s_ss, s_rs, t_ss, t_rs, e_ss, e_rs,
+):
+    ctx = lax.axis_index("ctx")
+    head = lax.axis_index("head")
+    zi, yi = ctx // 2, ctx % 2
+    rows = tokens.shape[0]
+    depth = weight.shape[0]
+    slice_width = 2 * depth
+    quarter = rows // 4
+
+    def along_z(d):
+        return lax.rem(zi + d, nz)
+
+    def device_z(d):
+        return (along_z(d) * 2 + yi, head)
+
+    pair = (zi * 2 + 1 - yi, head)
+    core_peer = head + 1 - 2 * (head % 2)
+    x_peer = lax.rem(head + 2, 4)
+
+    def remote(src, dst, ss, rs, device):
+        return pltpu.make_async_remote_copy(
+            src_ref=src, dst_ref=dst, send_sem=ss, recv_sem=rs, device_id=device, device_id_type=MESH
+        )
+
+    def columns(z):
+        return pl.ds(pl.multiple_of(z * slice_width, 128), slice_width)
+
+    def token_rows(h):
+        return pl.ds(pl.multiple_of(h * quarter, quarter), quarter)
+
+    own_rows = pl.ds(pl.multiple_of(yi * depth, depth), depth)
+
+    own_tokens = pltpu.make_async_copy(tokens.at[:, columns(zi)], tok.at[zi], local_sem.at[0])
+    own_tokens.start()
+    own_weights = []
+    for j in range(chunks):
+        own_weights.append(
+            pltpu.make_async_copy(
+                weight.at[:, pl.ds(j * CW, CW)], wbuf.at[j, own_rows, :], local_sem.at[1 + j]
+            )
+        )
+        own_weights[j].start()
+
+    barrier = pltpu.get_barrier_semaphore()
+    greeted = [device_z(d) for d in range(1, nz)] + [pair, (ctx, core_peer), (ctx, x_peer)]
+    for device in greeted:
+        pl.semaphore_signal(barrier, inc=1, device_id=device, device_id_type=MESH)
+    pl.semaphore_wait(barrier, len(greeted))
+
+    token_copies = {}
+    for d in range(nz - 1, 0, -1):
+        token_copies[d] = remote(
+            tokens.at[token_rows(head), columns(along_z(d))],
+            tok.at[zi, token_rows(head), :],
+            tok_ss.at[d], tok_rs.at[d], device_z(d),
+        )
+        token_copies[d].start()
+    w_copies = []
+    for j in range(chunks):
+        w_copies.append(
+            remote(
+                weight.at[:, pl.ds(j * CW, CW)], wbuf.at[j, own_rows, :], w_ss.at[j], w_rs.at[j], pair
+            )
+        )
+        w_copies[j].start()
+
+    row = lax.broadcasted_iota(jnp.int32, (rows, rows), 0)
+    column = lax.broadcasted_iota(jnp.int32, (rows, rows), 1)
+    causal = column <= row
+    for hd in range(2 * chunks):
+        lanes = pl.ds(hd * HD, HD)
+        full = lax.dot_general(
+            query[:, lanes], key[:, lanes], (((1,), (1,)), ((), ())), preferred_element_type=F32
+        )
+        scores[hd] = jnp.where(causal, full, 0.0).astype(BF16)
+
+    x_copies, core_copies = {}, {}
+    order = list(range(1, nz))
+    for d in order:
+        source = lax.rem(zi - d + nz, nz)
+        mine = tok.at[source, token_rows(head), :]
+        token_copies[d].wait_recv()
+        x_copies[d] = remote(mine, mine, x_ss.at[d], x_rs.at[d], (ctx, x_peer))
+        x_copies[d].start()
+        core_copies[d, 0] = remote(mine, mine, core_ss.at[0, d], core_rs.at[0, d], (ctx, core_peer))
+        core_copies[d, 0].start()
+    for d in order:
+        source = lax.rem(zi - d + nz, nz)
+        other = tok.at[source, token_rows(x_peer), :]
+        x_copies[d].wait_recv()
+        core_copies[d, 1] = remote(other, other, core_ss.at[1, d], core_rs.at[1, d], (ctx, core_peer))
+        core_copies[d, 1].start()
+    for d in order:
+        core_copies[d, 0].wait_recv()
+        core_copies[d, 1].wait_recv()
+    own_tokens.wait()
+
+    p_copies = {}
+    for j in range(chunks):
+        own_weights[j].wait()
+        w_copies[j].wait_recv()
+        for d in range(nz - 1, 0, -1):
+            part = jnp.dot(tok[along_z(d)], wbuf[j], preferred_element_type=F32)
+            p_send[d - 1, j] = part.astype(BF16)
+            p_copies[d, j] = remote(
+                p_send.at[d - 1, j], p_recv.at[d - 1, j], p_ss.at[d - 1, j], p_rs.at[d - 1, j], device_z(d)
+            )
+            p_copies[d, j].start()
+        acc[j] = jnp.dot(tok[zi], wbuf[j], preferred_element_type=F32)
+
+    s_copies = [
+        remote(state.at[j, 1 - yi], state_in.at[j], s_ss.at[j], s_rs.at[j], pair) for j in range(chunks)
+    ]
+    e_copies = [
+        remote(pre_send.at[j], pre.at[j, yi], e_ss.at[j], e_rs.at[j], pair) for j in range(chunks)
+    ]
+
+    def t_copy(d, j):
+        return remote(t_send.at[j], t_recv.at[d - 1, j], t_ss.at[d - 1, j], t_rs.at[d - 1, j], device_z(d))
+
+    def values(j):
+        total = acc[j]
+        for d in range(1, nz):
+            p_copies[d, j].wait_recv()
+            total = total + p_recv[d - 1, j].astype(F32)
+        value[j] = (total / (1.0 + jnp.exp(-total))).astype(BF16)
+        for i in range(2):
+            hd = 2 * j + i
+            state[j, i] = lax.dot_general(
+                key[:, pl.ds(hd * HD, HD)], value[j, :, pl.ds(i * HD, HD)],
+                (((0,), (0,)), ((), ())), preferred_element_type=F32,
+            )
+        s_copies[j].start()
+        for i in range(2):
+            att[2 * j + i] = jnp.dot(
+                scores[2 * j + i], value[j, :, pl.ds(i * HD, HD)], preferred_element_type=F32
+            )
+
+    def pair_sum(j):
+        s_copies[j].wait_recv()
+        t_send[j] = (state[j, yi] + state_in[j]).astype(BF16)
+        for d in range(1, nz):
+            @pl.when(zi + d < nz)
+            def _():
+                t_copy(d, j).start()
+
+    def earlier(j):
+        pre_send[j] = jnp.zeros((HD, HD), F32)
+        for d in range(1, nz):
+            @pl.when(zi - d >= 0)
+            def _():
+                t_copy(d, j).wait_recv()
+                pre_send[j] = pre_send[j] + t_recv[d - 1, j].astype(F32)
+        second = yi.astype(F32)
+        before = pre_send[j]
+        pre[j, yi] = before + second * state_in[j]
+        pre_send[j] = before + (1.0 - second) * state[j, yi]
+        e_copies[j].start()
+
+    def finish(j):
+        e_copies[j].wait_recv()
+        for i in range(2):
+            lanes = pl.ds((2 * j + i) * HD, HD)
+            whole = pre[j, i]
+            high = whole.astype(BF16)
+            low = (whole - high.astype(F32)).astype(BF16)
+            q = query[:, lanes]
+            attended = (
+                att[2 * j + i]
+                + jnp.dot(q, high, preferred_element_type=F32)
+                + jnp.dot(q, low, preferred_element_type=F32)
+            )
+            mean_square = jnp.mean(attended * attended, axis=1, keepdims=True)
+            out[:, lanes] = (attended * lax.rsqrt(mean_square + 1e-05) * gain[:, lanes]).astype(BF16)
+
+    stages = (values, pair_sum, earlier, finish)
+    for step in range(chunks + len(stages) - 1):
+        for lag, stage in enumerate(stages):
+            if 0 <= step - lag < chunks:
+                stage(step - lag)
+
+    for copy in [*token_copies.values(), *w_copies, *x_copies.values(), *core_copies.values()]:
+        copy.wait_send()
+    for copy in [*p_copies.values(), *s_copies, *e_copies]:
+        copy.wait_send()
+    for j in range(chunks):
+        for d in range(1, nz):
+            @pl.when(zi + d < nz)
+            def _():
+                t_copy(d, j).wait_send()
+
+
+def fused(n, tokens, query, key, weight, gain):
+    rows = tokens.shape[0]
+    depth, width = weight.shape
+    nz = n // 2
+    chunks = width // CW
+    dma = pltpu.SemaphoreType.DMA
+    hbm = pl.BlockSpec(memory_space=pl.ANY)
+    vmem = pl.BlockSpec(memory_space=pltpu.VMEM)
+    others = nz - 1
+    return pl.pallas_call(
+        functools.partial(fused_kernel, nz, chunks),
+        out_shape=jax.ShapeDtypeStruct((rows, width), BF16),
+        in_specs=[hbm, vmem, vmem, hbm, vmem],
+        out_specs=vmem,
+        scratch_shapes=[
+            pltpu.VMEM((nz, rows, 2 * depth), BF16),
+            pltpu.VMEM((chunks, 2 * depth, CW), BF16),
+            pltpu.VMEM((others, chunks, rows, CW), BF16),
+            pltpu.VMEM((others, chunks, rows, CW), BF16),
+            pltpu.VMEM((chunks, rows, CW), F32),
+            pltpu.VMEM((2 * chunks, rows, rows), BF16),
+            pltpu.VMEM((chunks, rows, CW), BF16),
+            pltpu.VMEM((2 * chunks, rows, HD), F32),
+            pltpu.VMEM((chunks, 2, HD, HD), F32),
+            pltpu.VMEM((chunks, HD, HD), F32),
+            pltpu.VMEM((chunks, HD, HD), BF16),
+            pltpu.VMEM((others, chunks, HD, HD), BF16),
+            pltpu.VMEM((chunks, HD, HD), F32),
+            pltpu.VMEM((chunks, 2, HD, HD), F32),
+            dma((1 + chunks,)),
+            dma((chunks,)), dma((chunks,)),
+            dma((nz,)), dma((nz,)),
+            dma((nz,)), dma((nz,)),
+            dma((2, nz)), dma((2, nz)),
+            dma((others, chunks)), dma((others, chunks)),
+            dma((chunks,)), dma((chunks,)),
+            dma((others, chunks)), dma((others, chunks)),
+            dma((chunks,)), dma((chunks,)),
+        ],
+        compiler_params=pltpu.CompilerParams(
+            collective_id=0, has_side_effects=True, vmem_limit_bytes=48 << 20
+        ),
+    )(tokens, query, key, weight, gain.reshape(1, width))
+
+
+def on_device(n, heads, tokens, query_heads, key_heads, w_value, norm_gain):
+    rows = tokens.shape[0]
+    depth, width = w_value.shape
+    fits = n % 2 == 0 and heads == 4 and rows == BLOCK and depth % 128 == 0 and width % CW == 0 and n <= 16
+    if fits:
+        return fused(n, tokens, query_heads, key_heads, w_value, norm_gain)
+    return plain(tokens, query_heads, key_heads, w_value, norm_gain)
+
+
 def solution(mesh):
     return jax.shard_map(
-        on_device,
+        functools.partial(on_device, mesh.shape["ctx"], mesh.shape["head"]),
         mesh=mesh,
         in_specs=(P("ctx", None), P("ctx", "head"), P("ctx", "head"), P("ctx", "head"), P("head")),
         out_specs=P("ctx", "head"),

time: 306 us -> 103 us (0.34)
  the two profiles are of different devices: /device:TPU:31 before, /device:TPU:29 now
where the time goes in v1:
time: 103 us; the launch traced here: 102 us
  Pallas kernels  97.5 us (95%)
  local copies, waits for them, and re-layouts  4.97 us (5%)
    pallas_call x1, Pallas kernels, fused(): pl.pallas_call(functools.partial(fused_kernel, nz, chunks), out_shape=jax...  97.5 us
    unnamed x9, local copies, waits for them, and re-layouts  4.97 us

profile of v1, /device:TPU:29, one launch (start us, length us, event | category | flops | bytes accessed | tf_op | source)
XLA Modules:
  0.0 102.5 jit_solution(10340247000458682778)
XLA Ops:
  0.0 0.0 copy-start
  0.0 1.4 %copy-done = bf16[768,1024]{1,0:T(8,128)(2,1)S(1)} copy-done((bf16[768,1024]{1,0:T(8,128)(2,1)S(1)}, bf16[768,1024]{1,0:T(8,128)(2,1)}, u32[]{:S(2)}) %copy-start) | copy-done | bytes 1572888
  1.4 0.0 copy-start.1
  1.4 1.0 %copy-done.1 = bf16[256,1024]{1,0:T(8,128)(2,1)S(1)} copy-done((bf16[256,1024]{1,0:T(8,128)(2,1)S(1)}, bf16[256,1024]{1,0:T(8,128)(2,1)}, u32[]{:S(2)}) %copy-start.1) | copy-done | bytes 524312
  2.5 0.0 copy-start.2
  2.5 1.0 %copy-done.2 = bf16[256,1024]{1,0:T(8,128)(2,1)S(1)} copy-done((bf16[256,1024]{1,0:T(8,128)(2,1)S(1)}, bf16[256,1024]{1,0:T(8,128)(2,1)}, u32[]{:S(2)}) %copy-start.2) | copy-done | bytes 524312
  3.5 0.0 copy-start.3
  3.5 0.7 copy-done.3
  4.2 97.5 %shard_map.55 = bf16[256,1024]{1,0:T(8,128)(2,1)S(1)} custom-call(bf16[256,6144]{1,0:T(8,128)(2,1)} %tokens.1, bf16[256,1024]{1,0:T(8,128)(2,1)S(1)} %copy-done.1, bf16[256,1024]{1,0:T(8,128)(2,1)S(1)} %copy-done.2, bf16[768,1024]{1,0:T(8,128)(2,1)S(1)} %copy-done, f32[1,1024]{1,0:T(1,128)S(1)} %bitcast.1), custom_call_target="tpu_custom_call" | custom-call | tf_op jit(solution)/shard_map/pallas_call | solution.py:276
  101.7 0.8 copy.7
Async XLA Ops:
  0.0 1.4 %copy-start = (bf16[768,1024]{1,0:T(8,128)(2,1)S(1)}, bf16[768,1024]{1,0:T(8,128)(2,1)}, u32[]{:S(2)}) copy-start(bf16[768,1024]{1,0:T(8,128)(2,1)} %weight.1) | copy-start | bytes 4718596
  1.4 1.0 %copy-start.1 = (bf16[256,1024]{1,0:T(8,128)(2,1)S(1)}, bf16[256,1024]{1,0:T(8,128)(2,1)}, u32[]{:S(2)}) copy-start(bf16[256,1024]{1,0:T(8,128)(2,1)} %query.1) | copy-start | bytes 1572868
  2.5 1.0 %copy-start.2 = (bf16[256,1024]{1,0:T(8,128)(2,1)S(1)}, bf16[256,1024]{1,0:T(8,128)(2,1)}, u32[]{:S(2)}) copy-start(bf16[256,1024]{1,0:T(8,128)(2,1)} %key.1) | copy-start | bytes 1572868
  3.5 0.7 copy-start.3

commit v2 on v1

--- a/solution.py
+++ b/solution.py
@@ -11,6 +11,8 @@
 F32 = jnp.float32
 BF16 = jnp.bfloat16
 CW = 256
+W_AHEAD = 2
+ORDER = (1, 3, 2)
 
 HD = 128
 BLOCK = 256
@@ -69,9 +71,10 @@
 
 def fused_kernel(
     nz, chunks, tokens, query, key, weight, gain, out,
-    tok, wbuf, p_send, p_recv, acc, scores, value, att, state, state_in, t_send, t_recv, pre_send, pre,
-    local_sem, w_ss, w_rs, tok_ss, tok_rs, x_ss, x_rs, core_ss, core_rs, p_ss, p_rs,
-    s_ss, s_rs, t_ss, t_rs, e_ss, e_rs,
+    tok, wbuf, p_send, p_recv, far, far_send, far_recv, acc, scores, value, att,
+    state, state_in, t_send, u_send, t_recv, u_recv, pre_send, pre,
+    local_sem, w_ss, w_rs, tok_ss, tok_rs, x_ss, x_rs, core_ss, core_rs, p_ss, p_rs, f_ss, f_rs,
+    s_ss, s_rs, t_ss, t_rs, u_ss, u_rs, e_ss, e_rs,
 ):
     ctx = lax.axis_index("ctx")
     head = lax.axis_index("head")
@@ -81,11 +84,10 @@
     slice_width = 2 * depth
     quarter = rows // 4
 
-    def along_z(d):
-        return lax.rem(zi + d, nz)
-
-    def device_z(d):
-        return (along_z(d) * 2 + yi, head)
+    z_peers = {1: zi + 1 - 2 * (zi % 2), 2: lax.rem(zi + 2, nz), 3: nz - 1 - zi}
+
+    def device_z(m):
+        return (z_peers[m] * 2 + yi, head)
 
     pair = (zi * 2 + 1 - yi, head)
     core_peer = head + 1 - 2 * (head % 2)
@@ -116,19 +118,11 @@
         own_weights[j].start()
 
     barrier = pltpu.get_barrier_semaphore()
-    greeted = [device_z(d) for d in range(1, nz)] + [pair, (ctx, core_peer), (ctx, x_peer)]
+    greeted = [device_z(m) for m in z_peers] + [pair, (ctx, core_peer), (ctx, x_peer)]
     for device in greeted:
         pl.semaphore_signal(barrier, inc=1, device_id=device, device_id_type=MESH)
     pl.semaphore_wait(barrier, len(greeted))
 
-    token_copies = {}
-    for d in range(nz - 1, 0, -1):
-        token_copies[d] = remote(
-            tokens.at[token_rows(head), columns(along_z(d))],
-            tok.at[zi, token_rows(head), :],
-            tok_ss.at[d], tok_rs.at[d], device_z(d),
-        )
-        token_copies[d].start()
     w_copies = []
     for j in range(chunks):
         w_copies.append(
@@ -136,7 +130,16 @@
                 weight.at[:, pl.ds(j * CW, CW)], wbuf.at[j, own_rows, :], w_ss.at[j], w_rs.at[j], pair
             )
         )
+    for j in range(min(W_AHEAD, chunks)):
         w_copies[j].start()
+    token_copies = {}
+    for m in ORDER:
+        token_copies[m] = remote(
+            tokens.at[token_rows(head), columns(z_peers[m])],
+            tok.at[zi, token_rows(head), :],
+            tok_ss.at[m], tok_rs.at[m], device_z(m),
+        )
+        token_copies[m].start()
 
     row = lax.broadcasted_iota(jnp.int32, (rows, rows), 0)
     column = lax.broadcasted_iota(jnp.int32, (rows, rows), 1)
@@ -149,38 +152,53 @@
         scores[hd] = jnp.where(causal, full, 0.0).astype(BF16)
 
     x_copies, core_copies = {}, {}
-    order = list(range(1, nz))
-    for d in order:
-        source = lax.rem(zi - d + nz, nz)
-        mine = tok.at[source, token_rows(head), :]
-        token_copies[d].wait_recv()
-        x_copies[d] = remote(mine, mine, x_ss.at[d], x_rs.at[d], (ctx, x_peer))
-        x_copies[d].start()
-        core_copies[d, 0] = remote(mine, mine, core_ss.at[0, d], core_rs.at[0, d], (ctx, core_peer))
-        core_copies[d, 0].start()
-    for d in order:
-        source = lax.rem(zi - d + nz, nz)
-        other = tok.at[source, token_rows(x_peer), :]
-        x_copies[d].wait_recv()
-        core_copies[d, 1] = remote(other, other, core_ss.at[1, d], core_rs.at[1, d], (ctx, core_peer))
-        core_copies[d, 1].start()
-    for d in order:
-        core_copies[d, 0].wait_recv()
-        core_copies[d, 1].wait_recv()
-    own_tokens.wait()
-
-    p_copies = {}
-    for j in range(chunks):
+    for m in ORDER:
+        mine = tok.at[z_peers[m], token_rows(head), :]
+        token_copies[m].wait_recv()
+        x_copies[m] = remote(mine, mine, x_ss.at[m], x_rs.at[m], (ctx, x_peer))
+        x_copies[m].start()
+        core_copies[m, 0] = remote(mine, mine, core_ss.at[0, m], core_rs.at[0, m], (ctx, core_peer))
+        core_copies[m, 0].start()
+    for m in ORDER:
+        other = tok.at[z_peers[m], token_rows(x_peer), :]
+        x_copies[m].wait_recv()
+        core_copies[m, 1] = remote(other, other, core_ss.at[1, m], core_rs.at[1, m], (ctx, core_peer))
+        core_copies[m, 1].start()
+
+    p_copies = [remote(p_send.at[j], p_recv.at[j], p_ss.at[j], p_rs.at[j], device_z(1)) for j in range(chunks)]
+    far_copies = [
+        remote(far_send.at[j], far_recv.at[j], f_ss.at[j], f_rs.at[j], device_z(2)) for j in range(chunks)
+    ]
+
+    def tokens_of(m, j):
+        if j == 0:
+            core_copies[m, 0].wait_recv()
+            core_copies[m, 1].wait_recv()
+        return tok[z_peers[m]]
+
+    def near_parts(j):
         own_weights[j].wait()
         w_copies[j].wait_recv()
-        for d in range(nz - 1, 0, -1):
-            part = jnp.dot(tok[along_z(d)], wbuf[j], preferred_element_type=F32)
-            p_send[d - 1, j] = part.astype(BF16)
-            p_copies[d, j] = remote(
-                p_send.at[d - 1, j], p_recv.at[d - 1, j], p_ss.at[d - 1, j], p_rs.at[d - 1, j], device_z(d)
-            )
-            p_copies[d, j].start()
+        if j + W_AHEAD < chunks:
+            w_copies[j + W_AHEAD].start()
+        for i, m in enumerate((1, 3)):
+            p_send[j, i] = jnp.dot(tokens_of(m, j), wbuf[j], preferred_element_type=F32).astype(BF16)
+        p_copies[j].start()
+        if j == 0:
+            own_tokens.wait()
+        far[j] = jnp.dot(tokens_of(2, j), wbuf[j], preferred_element_type=F32)
         acc[j] = jnp.dot(tok[zi], wbuf[j], preferred_element_type=F32)
+
+    def far_parts(j):
+        p_copies[j].wait_recv()
+        far_send[j] = (far[j] + p_recv[j, 1].astype(F32)).astype(BF16)
+        far_copies[j].start()
+
+    for step in range(chunks + 1):
+        if step < chunks:
+            near_parts(step)
+        if step >= 1:
+            far_parts(step - 1)
 
     s_copies = [
         remote(state.at[j, 1 - yi], state_in.at[j], s_ss.at[j], s_rs.at[j], pair) for j in range(chunks)
@@ -189,14 +207,15 @@
         remote(pre_send.at[j], pre.at[j, yi], e_ss.at[j], e_rs.at[j], pair) for j in range(chunks)
     ]
 
-    def t_copy(d, j):
-        return remote(t_send.at[j], t_recv.at[d - 1, j], t_ss.at[d - 1, j], t_rs.at[d - 1, j], device_z(d))
+    t_copies = [remote(t_send.at[j], t_recv.at[j], t_ss.at[j], t_rs.at[j], device_z(1)) for j in range(chunks)]
+    u_copies = {
+        (m, j): remote(u_send.at[j], u_recv.at[j], u_ss.at[m, j], u_rs.at[j], device_z(m))
+        for m in (2, 3) for j in range(chunks)
+    }
 
     def values(j):
-        total = acc[j]
-        for d in range(1, nz):
-            p_copies[d, j].wait_recv()
-            total = total + p_recv[d - 1, j].astype(F32)
+        far_copies[j].wait_recv()
+        total = acc[j] + p_recv[j, 0].astype(F32) + far_recv[j].astype(F32)
         value[j] = (total / (1.0 + jnp.exp(-total))).astype(BF16)
         for i in range(2):
             hd = 2 * j + i
@@ -212,19 +231,31 @@
 
     def pair_sum(j):
         s_copies[j].wait_recv()
-        t_send[j] = (state[j, yi] + state_in[j]).astype(BF16)
-        for d in range(1, nz):
-            @pl.when(zi + d < nz)
-            def _():
-                t_copy(d, j).start()
+        pre_send[j] = jnp.zeros((HD, HD), F32)
+
+        @pl.when(zi % 2 == 0)
+        def _():
+            t_send[j] = (state[j, yi] + state_in[j]).astype(BF16)
+            t_copies[j].start()
+
+    def row_sum(j):
+        @pl.when(zi % 2 == 1)
+        def _():
+            t_copies[j].wait_recv()
+            pre_send[j] = t_recv[j].astype(F32)
+
+        @pl.when(zi == 1)
+        def _():
+            u_send[j] = (pre_send[j] + state[j, yi] + state_in[j]).astype(BF16)
+            u_copies[2, j].start()
+            u_copies[3, j].start()
 
     def earlier(j):
-        pre_send[j] = jnp.zeros((HD, HD), F32)
-        for d in range(1, nz):
-            @pl.when(zi - d >= 0)
-            def _():
-                t_copy(d, j).wait_recv()
-                pre_send[j] = pre_send[j] + t_recv[d - 1, j].astype(F32)
+        @pl.when(zi >= 2)
+        def _():
+            u_copies[2, j].wait_recv()
+            pre_send[j] = pre_send[j] + u_recv[j].astype(F32)
+
         second = yi.astype(F32)
         before = pre_send[j]
         pre[j, yi] = before + second * state_in[j]
@@ -247,7 +278,7 @@
             mean_square = jnp.mean(attended * attended, axis=1, keepdims=True)
             out[:, lanes] = (attended * lax.rsqrt(mean_square + 1e-05) * gain[:, lanes]).astype(BF16)
 
-    stages = (values, pair_sum, earlier, finish)
+    stages = (values, pair_sum, row_sum, earlier, finish)
     for step in range(chunks + len(stages) - 1):
         for lag, stage in enumerate(stages):
             if 0 <= step - lag < chunks:
@@ -255,13 +286,18 @@
 
     for copy in [*token_copies.values(), *w_copies, *x_copies.values(), *core_copies.values()]:
         copy.wait_send()
-    for copy in [*p_copies.values(), *s_copies, *e_copies]:
+    for copy in [*p_copies, *far_copies, *s_copies, *e_copies]:
         copy.wait_send()
-    for j in range(chunks):
-        for d in range(1, nz):
-            @pl.when(zi + d < nz)
-            def _():
-                t_copy(d, j).wait_send()
+
+    @pl.when(zi % 2 == 0)
+    def _():
+        for copy in t_copies:
+            copy.wait_send()
+
+    @pl.when(zi == 1)
+    def _():
+        for copy in u_copies.values():
+            copy.wait_send()
 
 
 def fused(n, tokens, query, key, weight, gain):
@@ -272,7 +308,6 @@
     dma = pltpu.SemaphoreType.DMA
     hbm = pl.BlockSpec(memory_space=pl.ANY)
     vmem = pl.BlockSpec(memory_space=pltpu.VMEM)
-    others = nz - 1
     return pl.pallas_call(
         functools.partial(fused_kernel, nz, chunks),
         out_shape=jax.ShapeDtypeStruct((rows, width), BF16),
@@ -281,8 +316,11 @@
         scratch_shapes=[
             pltpu.VMEM((nz, rows, 2 * depth), BF16),
             pltpu.VMEM((chunks, 2 * depth, CW), BF16),
-            pltpu.VMEM((others, chunks, rows, CW), BF16),
-            pltpu.VMEM((others, chunks, rows, CW), BF16),
+            pltpu.VMEM((chunks, 2, rows, CW), BF16),
+            pltpu.VMEM((chunks, 2, rows, CW), BF16),
+            pltpu.VMEM((chunks, rows, CW), F32),
+            pltpu.VMEM((chunks, rows, CW), BF16),
+            pltpu.VMEM((chunks, rows, CW), BF16),
             pltpu.VMEM((chunks, rows, CW), F32),
             pltpu.VMEM((2 * chunks, rows, rows), BF16),
             pltpu.VMEM((chunks, rows, CW), BF16),
@@ -290,7 +328,9 @@
             pltpu.VMEM((chunks, 2, HD, HD), F32),
             pltpu.VMEM((chunks, HD, HD), F32),
             pltpu.VMEM((chunks, HD, HD), BF16),
-            pltpu.VMEM((others, chunks, HD, HD), BF16),
+            pltpu.VMEM((chunks, HD, HD), BF16),
+            pltpu.VMEM((chunks, HD, HD), BF16),
+            pltpu.VMEM((chunks, HD, HD), BF16),
             pltpu.VMEM((chunks, HD, HD), F32),
             pltpu.VMEM((chunks, 2, HD, HD), F32),
             dma((1 + chunks,)),
@@ -298,9 +338,11 @@
             dma((nz,)), dma((nz,)),
             dma((nz,)), dma((nz,)),
             dma((2, nz)), dma((2, nz)),
-            dma((others, chunks)), dma((others, chunks)),
-            dma((chunks,)), dma((chunks,)),
-            dma((others, chunks)), dma((others, chunks)),
+            dma((chunks,)), dma((chunks,)),
+            dma((chunks,)), dma((chunks,)),
+            dma((chunks,)), dma((chunks,)),
+            dma((chunks,)), dma((chunks,)),
+            dma((nz, chunks)), dma((chunks,)),
             dma((chunks,)), dma((chunks,)),
         ],
         compiler_params=pltpu.CompilerParams(
@@ -312,7 +354,7 @@
 def on_device(n, heads, tokens, query_heads, key_heads, w_value, norm_gain):
     rows = tokens.shape[0]
     depth, width = w_value.shape
-    fits = n % 2 == 0 and heads == 4 and rows == BLOCK and depth % 128 == 0 and width % CW == 0 and n <= 16
+    fits = n == 8 and heads == 4 and rows == BLOCK and depth % 128 == 0 and width % CW == 0
     if fits:
         return fused(n, tokens, query_heads, key_heads, w_value, norm_gain)
     return plain(tokens, query_heads, key_heads, w_value, norm_gain)

time: 103 us -> 84.5 us (0.82)
  the two profiles are of different devices: /device:TPU:29 before, /device:TPU:0 now
where the time goes in v2:
time: 84.5 us; the launch traced here: 84.2 us
  Pallas kernels  79.2 us (94%)
  local copies, waits for them, and re-layouts  4.97 us (6%)
    pallas_call x1, Pallas kernels, fused(): pl.pallas_call(functools.partial(fused_kernel, nz, chunks), out_shape=jax...  79.2 us
    unnamed x9, local copies, waits for them, and re-layouts  4.97 us

profile of v2, /device:TPU:0, one launch (start us, length us, event | category | flops | bytes accessed | tf_op | source)
XLA Modules:
  0.0 84.2 jit_solution(10329736377002465736)
XLA Ops:
  0.0 0.0 copy-start
  0.0 1.4 %copy-done = bf16[768,1024]{1,0:T(8,128)(2,1)S(1)} copy-done((bf16[768,1024]{1,0:T(8,128)(2,1)S(1)}, bf16[768,1024]{1,0:T(8,128)(2,1)}, u32[]{:S(2)}) %copy-start) | copy-done | bytes 1572888
  1.4 0.0 copy-start.1
  1.4 1.0 %copy-done.1 = bf16[256,1024]{1,0:T(8,128)(2,1)S(1)} copy-done((bf16[256,1024]{1,0:T(8,128)(2,1)S(1)}, bf16[256,1024]{1,0:T(8,128)(2,1)}, u32[]{:S(2)}) %copy-start.1) | copy-done | bytes 524312
  2.5 0.0 copy-start.2
  2.5 1.0 %copy-done.2 = bf16[256,1024]{1,0:T(8,128)(2,1)S(1)} copy-done((bf16[256,1024]{1,0:T(8,128)(2,1)S(1)}, bf16[256,1024]{1,0:T(8,128)(2,1)}, u32[]{:S(2)}) %copy-start.2) | copy-done | bytes 524312
  3.5 0.0 copy-start.3
  3.5 0.7 copy-done.3
  4.2 79.2 %shard_map.55 = bf16[256,1024]{1,0:T(8,128)(2,1)S(1)} custom-call(bf16[256,6144]{1,0:T(8,128)(2,1)} %tokens.1, bf16[256,1024]{1,0:T(8,128)(2,1)S(1)} %copy-done.1, bf16[256,1024]{1,0:T(8,128)(2,1)S(1)} %copy-done.2, bf16[768,1024]{1,0:T(8,128)(2,1)S(1)} %copy-done, f32[1,1024]{1,0:T(1,128)S(1)} %bitcast.1), custom_call_target="tpu_custom_call" | custom-call | tf_op jit(solution)/shard_map/pallas_call | solution.py:311
  83.4 0.8 copy.7
Async XLA Ops:
  0.0 1.4 %copy-start = (bf16[768,1024]{1,0:T(8,128)(2,1)S(1)}, bf16[768,1024]{1,0:T(8,128)(2,1)}, u32[]{:S(2)}) copy-start(bf16[768,1024]{1,0:T(8,128)(2,1)} %weight.1) | copy-start | bytes 4718596
  1.4 1.0 %copy-start.1 = (bf16[256,1024]{1,0:T(8,128)(2,1)S(1)}, bf16[256,1024]{1,0:T(8,128)(2,1)}, u32[]{:S(2)}) copy-start(bf16[256,1024]{1,0:T(8,128)(2,1)} %query.1) | copy-start | bytes 1572868
  2.5 1.0 %copy-start.2 = (bf16[256,1024]{1,0:T(8,128)(2,1)S(1)}, bf16[256,1024]{1,0:T(8,128)(2,1)}, u32[]{:S(2)}) copy-start(bf16[256,1024]{1,0:T(8,128)(2,1)} %key.1) | copy-start | bytes 1572868
  3.5 0.7 copy-start.3

commit v3 on v2

--- a/solution.py
+++ b/solution.py
@@ -194,12 +194,6 @@
         far_send[j] = (far[j] + p_recv[j, 1].astype(F32)).astype(BF16)
         far_copies[j].start()
 
-    for step in range(chunks + 1):
-        if step < chunks:
-            near_parts(step)
-        if step >= 1:
-            far_parts(step - 1)
-
     s_copies = [
         remote(state.at[j, 1 - yi], state_in.at[j], s_ss.at[j], s_rs.at[j], pair) for j in range(chunks)
     ]
@@ -278,9 +272,9 @@
             mean_square = jnp.mean(attended * attended, axis=1, keepdims=True)
             out[:, lanes] = (attended * lax.rsqrt(mean_square + 1e-05) * gain[:, lanes]).astype(BF16)
 
-    stages = (values, pair_sum, row_sum, earlier, finish)
-    for step in range(chunks + len(stages) - 1):
-        for lag, stage in enumerate(stages):
+    stages = {near_parts: 0, far_parts: 1, values: 2, pair_sum: 3, row_sum: 4, earlier: 5, finish: 6}
+    for step in range(chunks + stages[finish]):
+        for stage, lag in stages.items():
             if 0 <= step - lag < chunks:
                 stage(step - lag)
 

time: 84.5 us -> 83.2 us (0.985)
  Pallas kernels: 79.2 us -> 77.9 us
    pallas_call x1, Pallas kernels: 79.2 us -> 77.9 us  [fused(): pl.pallas_call(functools.partial(fused_kernel, nz, chunks), out_shape=jax...]
where the time goes in v3:
time: 83.2 us; the launch traced here: 82.9 us
  Pallas kernels  77.9 us (94%)
  local copies, waits for them, and re-layouts  4.97 us (6%)
    pallas_call x1, Pallas kernels, fused(): pl.pallas_call(functools.partial(fused_kernel, nz, chunks), out_shape=jax...  77.9 us
    unnamed x9, local copies, waits for them, and re-layouts  4.97 us

profile of v3, /device:TPU:0, one launch (start us, length us, event | category | flops | bytes accessed | tf_op | source)
XLA Modules:
  0.0 82.9 jit_solution(15081252300306948367)
XLA Ops:
  0.0 0.0 copy-start
  0.0 1.4 %copy-done = bf16[768,1024]{1,0:T(8,128)(2,1)S(1)} copy-done((bf16[768,1024]{1,0:T(8,128)(2,1)S(1)}, bf16[768,1024]{1,0:T(8,128)(2,1)}, u32[]{:S(2)}) %copy-start) | copy-done | bytes 1572888
  1.4 0.0 copy-start.1
  1.4 1.0 %copy-done.1 = bf16[256,1024]{1,0:T(8,128)(2,1)S(1)} copy-done((bf16[256,1024]{1,0:T(8,128)(2,1)S(1)}, bf16[256,1024]{1,0:T(8,128)(2,1)}, u32[]{:S(2)}) %copy-start.1) | copy-done | bytes 524312
  2.5 0.0 copy-start.2
  2.5 1.0 %copy-done.2 = bf16[256,1024]{1,0:T(8,128)(2,1)S(1)} copy-done((bf16[256,1024]{1,0:T(8,128)(2,1)S(1)}, bf16[256,1024]{1,0:T(8,128)(2,1)}, u32[]{:S(2)}) %copy-start.2) | copy-done | bytes 524312
  3.5 0.0 copy-start.3
  3.5 0.7 copy-done.3
  4.2 77.9 %shard_map.55 = bf16[256,1024]{1,0:T(8,128)(2,1)S(1)} custom-call(bf16[256,6144]{1,0:T(8,128)(2,1)} %tokens.1, bf16[256,1024]{1,0:T(8,128)(2,1)S(1)} %copy-done.1, bf16[256,1024]{1,0:T(8,128)(2,1)S(1)} %copy-done.2, bf16[768,1024]{1,0:T(8,128)(2,1)S(1)} %copy-done, f32[1,1024]{1,0:T(1,128)S(1)} %bitcast.1), custom_call_target="tpu_custom_call" | custom-call | tf_op jit(solution)/shard_map/pallas_call | solution.py:305
  82.1 0.8 copy.7
Async XLA Ops:
  0.0 1.4 %copy-start = (bf16[768,1024]{1,0:T(8,128)(2,1)S(1)}, bf16[768,1024]{1,0:T(8,128)(2,1)}, u32[]{:S(2)}) copy-start(bf16[768,1024]{1,0:T(8,128)(2,1)} %weight.1) | copy-start | bytes 4718596
  1.4 1.0 %copy-start.1 = (bf16[256,1024]{1,0:T(8,128)(2,1)S(1)}, bf16[256,1024]{1,0:T(8,128)(2,1)}, u32[]{:S(2)}) copy-start(bf16[256,1024]{1,0:T(8,128)(2,1)} %query.1) | copy-start | bytes 1572868
  2.5 1.0 %copy-start.2 = (bf16[256,1024]{1,0:T(8,128)(2,1)S(1)}, bf16[256,1024]{1,0:T(8,128)(2,1)}, u32[]{:S(2)}) copy-start(bf16[256,1024]{1,0:T(8,128)(2,1)} %key.1) | copy-start | bytes 1572868
  3.5 0.7 copy-start.3
